TPU v7x, 32 devices: a whole 2x2x4 slice. The times are simulated.
32 devices in a mesh: rep: 16 (over z, y, core), fsdp: 2 (over x).
Axes of the slice: x: 2, y: 2, z: 4, core: 2. Of those that a mesh axis runs over, the one named last changes fastest.
Arguments:
- activations: bfloat16 [16, 1024, 1600], P('rep', 'fsdp'), may hold values from -6 to 6
- segments: int32 [16, 1024], P('rep'), may hold values from 0 to 4, never falling along the last dimension, each value on 1 to 512 neighbouring positions
- attend_gain: bfloat16 [1600], P('fsdp'), may hold values from 0.5 to 1.5
- attend_shift: bfloat16 [1600], P('fsdp'), may hold values from -3 to 3
- input_weight: bfloat16 [1600, 4800], P('fsdp'), may hold values from -0.15625 to 0.15625
- input_bias: bfloat16 [3200], P('fsdp'), may hold values from -3 to 3
- output_weight: bfloat16 [1600, 1600], P('fsdp'), may hold values from -0.625 to 0.625
- output_bias: bfloat16 [1600], P('fsdp'), may hold values from -3 to 3
- dense_gain: bfloat16 [1600], P('fsdp'), may hold values from 0.5 to 1.5
- dense_shift: bfloat16 [1600], P('fsdp'), may hold values from -3 to 3
- expand_weight: bfloat16 [1600, 6400], P('fsdp'), may hold values from -0.15625 to 0.15625
- expand_bias: bfloat16 [6400], P('fsdp'), may hold values from -3 to 3
- reduce_weight: bfloat16 [6400, 1600], P('fsdp'), may hold values from -0.078125 to 0.078125
- reduce_bias: bfloat16 [1600], P('fsdp'), may hold values from -3 to 3
- cotangent: bfloat16 [16, 1024, 1600], P('rep', 'fsdp'), may hold values from -6 to 6
Outputs:
- outputs: bfloat16 [16, 1024, 1600], P('rep', 'fsdp')
- activations_grad: bfloat16 [16, 1024, 1600], P('rep', 'fsdp')
- attend_gain_grad: float32 [1600], P('fsdp')
- attend_shift_grad: float32 [1600], P('fsdp')
- input_weight_grad: float32 [1600, 4800], P('fsdp', 'rep')
- input_bias_grad: float32 [3200], P('fsdp')
- output_weight_grad: float32 [1600, 1600], P('fsdp', 'rep')
- output_bias_grad: float32 [1600], P('fsdp')
- dense_gain_grad: float32 [1600], P('fsdp')
- dense_shift_grad: float32 [1600], P('fsdp')
- expand_weight_grad: float32 [1600, 6400], P('fsdp', 'rep')
- expand_bias_grad: float32 [6400], P('fsdp')
- reduce_weight_grad: float32 [6400, 1600], P('fsdp', 'rep')
- reduce_bias_grad: float32 [1600], P('fsdp')
Inputs may be any that keep to these rules, and one draw needn't show every extreme that they name: `segments`: along each group the ids never fall and each of the 5 ids occurs; id 0 is the group's prompt, the others its continuations.
All inputs are finite; a program needn't handle non-finite values.
Results may differ from a plain program's by a relative error of at most 0.018.
Values may be sent and summed in bfloat16 or wider, within the bound.
A program may use at most 384 MiB of HBM per device.

v0:
```python
import jax
import jax.numpy as jnp
from jax import lax
from jax.sharding import PartitionSpec as P

HEADS = 25
HEAD_DIM = 64


norm_eps = 1e-05
masked_score = -1e30


def layer_norm(values, gain, shift):
    average = jnp.mean(values, axis=-1, keepdims=True)
    centered = values - average
    variance = jnp.mean(centered * centered, axis=-1, keepdims=True)
    return centered * lax.rsqrt(variance + norm_eps) * gain + shift


def gelu_tanh(values):
    return jax.nn.gelu(values, approximate=True)


def local(
    activations,
    segments,
    attend_gain,
    attend_shift,
    input_weight,
    input_bias,
    output_weight,
    output_bias,
    dense_gain,
    dense_shift,
    expand_weight,
    expand_bias,
    reduce_weight,
    reduce_bias,
    cotangent,
):
    floating = jnp.float32
    brain = jnp.bfloat16
    tokens = activations[0].astype(floating)
    local_rows = tokens.shape[0]
    width = tokens.shape[1]
    first_token = lax.axis_index("fsdp") * local_rows
    segment_row = segments[0]
    score_scale = HEAD_DIM ** (-0.5)
    query_positions = first_token + jnp.arange(local_rows, dtype=jnp.int32)
    key_positions = jnp.arange(segment_row.shape[0], dtype=jnp.int32)
    query_segments = lax.dynamic_slice_in_dim(segment_row, first_token, local_rows, 0)
    allowed = (key_positions[None, :] <= query_positions[:, None]) & (
        (segment_row[None, :] == 0) | (segment_row[None, :] == query_segments[:, None])
    )
    gathered_attend = (
        lax.all_gather(attend_gain, "fsdp", axis=0, tiled=True),
        lax.all_gather(attend_shift, "fsdp", axis=0, tiled=True),
        lax.all_gather(input_weight, "fsdp", axis=0, tiled=True),
        lax.all_gather(input_bias, "fsdp", axis=0, tiled=True),
        lax.all_gather(output_weight, "fsdp", axis=0, tiled=True),
        lax.all_gather(output_bias, "fsdp", axis=0, tiled=True),
    )
    first_gain = gathered_attend[0].astype(floating)
    first_shift = gathered_attend[1].astype(floating)
    mixing_bias = gathered_attend[3].astype(floating)
    after_bias = gathered_attend[5].astype(floating)
    normed_first = layer_norm(tokens, first_gain, first_shift)
    normed_low = normed_first.astype(brain)
    projected = jnp.dot(normed_low, gathered_attend[2], preferred_element_type=floating)
    queries = (projected[:, :width] + mixing_bias[:width]).astype(brain)
    own_keys = projected[:, width : 2 * width].astype(brain)
    own_values = (projected[:, 2 * width :] + mixing_bias[width:]).astype(brain)
    all_keys, all_values = (
        lax.all_gather(own_keys, "fsdp", axis=0, tiled=True),
        lax.all_gather(own_values, "fsdp", axis=0, tiled=True),
    )
    query_heads = queries.reshape(local_rows, HEADS, HEAD_DIM).transpose(1, 0, 2)
    key_heads = all_keys.reshape(-1, HEADS, HEAD_DIM).transpose(1, 0, 2)
    value_heads = all_values.reshape(-1, HEADS, HEAD_DIM).transpose(1, 0, 2)

    def head_scores(query_one, key_one):
        scores = (
            jnp.einsum("qd,kd->qk", query_one, key_one, preferred_element_type=floating)
            * score_scale
        )
        return jnp.where(allowed, scores, masked_score)

    def head_forward(pieces):
        query_one, key_one, value_one = pieces
        masked = head_scores(query_one, key_one)
        largest = jnp.max(masked, axis=-1, keepdims=True)
        exponent = jnp.exp(masked - largest)
        denominator = jnp.sum(exponent, axis=-1, keepdims=True)
        probabilities = exponent / denominator
        context_one = jnp.einsum(
            "qk,kd->qd", probabilities.astype(brain), value_one, preferred_element_type=floating
        )
        return (context_one, (largest + jnp.log(denominator))[:, 0])

    context_heads, log_total = lax.map(head_forward, (query_heads, key_heads, value_heads))
    context_low = context_heads.transpose(1, 0, 2).reshape(local_rows, width).astype(brain)
    attended = (
        jnp.dot(context_low, gathered_attend[4], preferred_element_type=floating) + after_bias
    )
    middle = tokens + attended
    gathered_dense = (
        lax.all_gather(dense_gain, "fsdp", axis=0, tiled=True),
        lax.all_gather(dense_shift, "fsdp", axis=0, tiled=True),
        lax.all_gather(expand_weight, "fsdp", axis=0, tiled=True),
        lax.all_gather(expand_bias, "fsdp", axis=0, tiled=True),
        lax.all_gather(reduce_weight, "fsdp", axis=0, tiled=True),
        lax.all_gather(reduce_bias, "fsdp", axis=0, tiled=True),
    )
    second_gain = gathered_dense[0].astype(floating)
    second_shift = gathered_dense[1].astype(floating)
    dense_normed = layer_norm(middle, second_gain, second_shift)
    dense_low = dense_normed.astype(brain)
    expanded = jnp.dot(
        dense_low, gathered_dense[2], preferred_element_type=floating
    ) + gathered_dense[3].astype(floating)
    activated_low = gelu_tanh(expanded).astype(brain)
    reduced = jnp.dot(
        activated_low, gathered_dense[4], preferred_element_type=floating
    ) + gathered_dense[5].astype(floating)
    outputs = (middle + reduced).astype(brain)[None]
    incoming_low = cotangent[0]
    incoming = incoming_low.astype(floating)
    dense_back = (
        lax.all_gather(dense_gain, "fsdp", axis=0, tiled=True),
        lax.all_gather(dense_shift, "fsdp", axis=0, tiled=True),
        lax.all_gather(expand_weight, "fsdp", axis=0, tiled=True),
        lax.all_gather(expand_bias, "fsdp", axis=0, tiled=True),
        lax.all_gather(reduce_weight, "fsdp", axis=0, tiled=True),
        lax.all_gather(reduce_bias, "fsdp", axis=0, tiled=True),
    )
    reduce_rows = lax.psum_scatter(
        jnp.einsum(
            "tr,td->rd", activated_low, incoming_low, preferred_element_type=floating
        ).astype(jnp.bfloat16),
        "fsdp",
        scatter_dimension=0,
        tiled=True,
    )
    activated_grad = jnp.einsum(
        "td,fd->tf", incoming_low, dense_back[4], preferred_element_type=floating
    )
    unused_value, gelu_pull = jax.vjp(gelu_tanh, expanded)
    expanded_grad = gelu_pull(activated_grad)[0].astype(brain)
    expand_rows = lax.psum_scatter(
        jnp.einsum("tr,tf->rf", dense_low, expanded_grad, preferred_element_type=floating).astype(
            jnp.bfloat16
        ),
        "fsdp",
        scatter_dimension=0,
        tiled=True,
    )
    dense_normed_grad = jnp.einsum(
        "tf,df->td", expanded_grad, dense_back[2], preferred_element_type=floating
    )
    unused_dense, dense_pull = jax.vjp(layer_norm, middle, second_gain, second_shift)
    middle_norm_grad, dense_gain_part, dense_shift_part = dense_pull(dense_normed_grad)
    middle_grad = incoming + middle_norm_grad
    attended_low = middle_grad.astype(brain)
    attend_back = (
        lax.all_gather(attend_gain, "fsdp", axis=0, tiled=True),
        lax.all_gather(attend_shift, "fsdp", axis=0, tiled=True),
        lax.all_gather(input_weight, "fsdp", axis=0, tiled=True),
        lax.all_gather(input_bias, "fsdp", axis=0, tiled=True),
        lax.all_gather(output_weight, "fsdp", axis=0, tiled=True),
        lax.all_gather(output_bias, "fsdp", axis=0, tiled=True),
    )
    output_rows = lax.psum_scatter(
        jnp.einsum("tr,td->rd", context_low, attended_low, preferred_element_type=floating).astype(
            jnp.bfloat16
        ),
        "fsdp",
        scatter_dimension=0,
        tiled=True,
    )
    context_grad = jnp.einsum(
        "te,de->td", attended_low, attend_back[4], preferred_element_type=floating
    )
    context_grad = (
        context_grad.astype(brain).reshape(local_rows, HEADS, HEAD_DIM).transpose(1, 0, 2)
    )

    def head_backward(pieces):
        query_one, key_one, value_one, grad_one, total_one = pieces
        masked = head_scores(query_one, key_one)
        probabilities = jnp.exp(masked - total_one[:, None])
        prob_grad = jnp.einsum("qd,kd->qk", grad_one, value_one, preferred_element_type=floating)
        value_one_grad = jnp.einsum(
            "qk,qd->kd", probabilities.astype(brain), grad_one, preferred_element_type=floating
        )
        score_grad = (
            probabilities * (prob_grad - jnp.sum(probabilities * prob_grad, axis=-1, keepdims=True))
        ).astype(brain)
        query_one_grad = (
            jnp.einsum("qk,kd->qd", score_grad, key_one, preferred_element_type=floating)
            * score_scale
        )
        key_one_grad = (
            jnp.einsum("qk,qd->kd", score_grad, query_one, preferred_element_type=floating)
            * score_scale
        )
        return (query_one_grad, key_one_grad, value_one_grad)

    query_stack, key_stack, value_stack = lax.map(
        head_backward, (query_heads, key_heads, value_heads, context_grad, log_total)
    )
    query_grad = query_stack.transpose(1, 0, 2).reshape(local_rows, width).astype(brain)
    key_part = key_stack.transpose(1, 0, 2).reshape(-1, width)
    value_part = value_stack.transpose(1, 0, 2).reshape(-1, width)
    (
        key_grad,
        value_grad,
        output_bias_grad,
        dense_gain_grad,
        dense_shift_grad,
        expand_bias_grad,
        reduce_bias_grad,
    ) = (
        lax.psum_scatter(key_part, "fsdp", scatter_dimension=0, tiled=True),
        lax.psum_scatter(value_part, "fsdp", scatter_dimension=0, tiled=True),
        lax.psum_scatter(
            jnp.sum(attended_low.astype(floating), axis=0), "fsdp", scatter_dimension=0, tiled=True
        ),
        lax.psum_scatter(dense_gain_part, "fsdp", scatter_dimension=0, tiled=True),
        lax.psum_scatter(dense_shift_part, "fsdp", scatter_dimension=0, tiled=True),
        lax.psum_scatter(
            jnp.sum(expanded_grad.astype(floating), axis=0), "fsdp", scatter_dimension=0, tiled=True
        ),
        lax.psum_scatter(jnp.sum(incoming, axis=0), "fsdp", scatter_dimension=0, tiled=True),
    )
    value_low = value_grad.astype(brain)
    mixed_grad = jnp.concatenate([query_grad, key_grad.astype(brain), value_low], axis=1)
    input_rows = lax.psum_scatter(
        jnp.einsum("tr,te->re", normed_low, mixed_grad, preferred_element_type=floating).astype(
            jnp.bfloat16
        ),
        "fsdp",
        scatter_dimension=0,
        tiled=True,
    )
    bias_part = jnp.concatenate(
        [jnp.sum(query_grad.astype(floating), axis=0), jnp.sum(value_low.astype(floating), axis=0)]
    )
    normed_grad = jnp.einsum(
        "te,de->td", mixed_grad, attend_back[2], preferred_element_type=floating
    )
    unused_first, first_pull = jax.vjp(layer_norm, tokens, first_gain, first_shift)
    token_norm_grad, attend_gain_part, attend_shift_part = first_pull(normed_grad)
    input_grads_out = (middle_grad + token_norm_grad).astype(brain)[None]
    attend_gain_grad, attend_shift_grad, input_bias_grad = (
        lax.psum_scatter(attend_gain_part, "fsdp", scatter_dimension=0, tiled=True),
        lax.psum_scatter(attend_shift_part, "fsdp", scatter_dimension=0, tiled=True),
        lax.psum_scatter(bias_part, "fsdp", scatter_dimension=0, tiled=True),
    )
    matrices = (
        lax.psum_scatter(input_rows, "rep", scatter_dimension=1, tiled=True).astype(jnp.float32),
        lax.psum_scatter(output_rows, "rep", scatter_dimension=1, tiled=True).astype(jnp.float32),
        lax.psum_scatter(expand_rows, "rep", scatter_dimension=1, tiled=True).astype(jnp.float32),
        lax.psum_scatter(reduce_rows, "rep", scatter_dimension=1, tiled=True).astype(jnp.float32),
    )
    smalls = lax.psum(
        (
            attend_gain_grad,
            attend_shift_grad,
            input_bias_grad,
            output_bias_grad,
            dense_gain_grad,
            dense_shift_grad,
            expand_bias_grad,
            reduce_bias_grad,
        ),
        "rep",
    )
    return (
        outputs,
        input_grads_out,
        smalls[0],
        smalls[1],
        matrices[0],
        smalls[2],
        matrices[1],
        smalls[3],
        smalls[4],
        smalls[5],
        matrices[2],
        smalls[6],
        matrices[3],
        smalls[7],
    )


def solution(mesh):
    in_specs = (
        P("rep", "fsdp", None),
        P("rep", None),
        P("fsdp"),
        P("fsdp"),
        P("fsdp", None),
        P("fsdp"),
        P("fsdp", None),
        P("fsdp"),
        P("fsdp"),
        P("fsdp"),
        P("fsdp", None),
        P("fsdp"),
        P("fsdp", None),
        P("fsdp"),
        P("rep", "fsdp", None),
    )
    out_specs = (
        P("rep", "fsdp", None),
        P("rep", "fsdp", None),
        P("fsdp"),
        P("fsdp"),
        P("fsdp", "rep"),
        P("fsdp"),
        P("fsdp", "rep"),
        P("fsdp"),
        P("fsdp"),
        P("fsdp"),
        P("fsdp", "rep"),
        P("fsdp"),
        P("fsdp", "rep"),
        P("fsdp"),
    )
    return jax.shard_map(local, mesh=mesh, in_specs=in_specs, out_specs=out_specs, check_vma=False)
```

profile of v0, /device:TPU:0, one launch (start us, length us, event | category | flops | bytes accessed | tf_op | source)
XLA Modules:
  0.0 2723.0 jit_solution(15711448115938316494)
XLA Ops:
  11.8 10.5 all-reduce.24
  23.7 174.0 %all-gather.8.cloned.1.call-done = bf16[1600,4800]{1,0:T(8,128)(2,1)} async-done(((bf16[800,4800]{1,0:T(8,128)(2,1)}), bf16[1600,4800]{1,0:T(8,128)(2,1)}) %all-gather.8.cloned.1.call-update) | async-done | bytes 15360016 | tf_op jit(solution)/shard_map/all_gather | solution.py:59
  197.7 15.3 fusion.83
  230.4 32.5 %all-gather.10.cloned.1.call-done = bf16[1024,1600]{0,1:T(8,128)(2,1)} async-done(((bf16[512,1600]{0,1:T(8,128)(2,1)}), bf16[1024,1600]{0,1:T(8,128)(2,1)}) %all-gather.10.cloned.1.call-update) | async-done | bytes 3276816 | tf_op jit(solution)/shard_map/all_gather | solution.py:75
  270.0 41.5 %all-gather.12.cloned.1.call-done = bf16[1024,1600]{0,1:T(8,128)(2,1)} async-done(((bf16[512,1600]{0,1:T(8,128)(2,1)}), bf16[1024,1600]{0,1:T(8,128)(2,1)}) %all-gather.12.cloned.1.call-update) | async-done | bytes 3276816 | tf_op jit(solution)/shard_map/all_gather | solution.py:76
  311.5 7.1 copy.38
  318.7 105.6 %while.28 = (s32[]{:T(128)}, bf16[25,512,64]{1,2,0:T(8,128)(2,1)S(1)}, f32[25,512]{1,0:T(8,128)S(1)}, bf16[25,512,64]{2,1,0:T(8,128)(2,1)}, bf16[25,1024,64]{2,1...) while((s32[]{:T(128)}, ...), condition=%wide.region_5.6_spmd.clone, body=%wide.region_2.5_spmd.clone.sunk | while | flops 140508672 | bytes 7109761 | solution.py:101
  433.1 192.7 %all-gather.16.cloned.1.call-done = bf16[1600,6400]{1,0:T(8,128)(2,1)} async-done(((bf16[800,6400]{1,0:T(8,128)(2,1)}), bf16[1600,6400]{1,0:T(8,128)(2,1)}) %all-gather.16.cloned.1.call-update) | async-done | bytes 20480016 | tf_op jit(solution)/shard_map/all_gather | solution.py:110
  625.8 21.2 convolution_add_fusion
  647.1 222.1 %all-gather.18.cloned.1.call-done = bf16[6400,1600]{0,1:T(8,128)(2,1)} async-done(((bf16[3200,1600]{0,1:T(8,128)(2,1)}), bf16[6400,1600]{0,1:T(8,128)(2,1)}) %all-gather.18.cloned.1.call-update) | async-done | bytes 20480016 | tf_op jit(solution)/shard_map/all_gather | solution.py:112
  869.2 29.9 %convert_reduce_fusion = (f32[6400]{0:T(1024)}, bf16[512,6400]{1,0:T(8,128)(2,1)}) fusion(f32[512,6400]{1,0:T(8,128)} %convolution_add_fusion, bf16[6400,1600]{0,1:T(8,128)(2,1)} %all-gather.18.cloned.1.call-done, bf16[1,512,1600]{1,2,0:T(8,128)(2,1)} %param.33), kind=kOutput, calls=%fused_computation.67 | convolution fusion | flops 10557843456 | bytes 41804800 | tf_op jit(solution)/shard_map/td,fd->tf/dot_general | solution.py:145
  899.1 21.4 multiply_reduce_fusion.1
  924.7 7.3 convolution_convert_fusion.4
  937.9 249.6 %while.29 = (s32[]{:T(128)}, bf16[25,512,64]{1,2,0:T(8,128)(2,1)}, f32[25,1024,64]{1,2,0:T(8,128)}, f32[25,1024,64]{1,2,0:T(8,128)}, bf16[25,512,64]{2,1,0:T(8,1...) while((s32[]{:T(128)}, bf16[25,512,64]{1,2,0:T(8,128)(2,1)}, ...), condition=%wide.region_12.13_spmd.clone, body=%wide.region_10.12_spmd.clone.sunk | while | flops 342457856 | bytes 17719440 | solution.py:209
  1188.7 7.5 convolution_convert_fusion.3
  1196.3 71.3 %reduce-scatter.16.cloned.1.call-done = f32[512,1600]{0,1:T(8,128)} async-done(((f32[1024,1600]{0,1:T(8,128)}), f32[512,1600]{0,1:T(8,128)}) %reduce-scatter.16.cloned.1.call-update) | async-done | bytes 3276816 | tf_op jit(solution)/shard_map/reduce_scatter | solution.py:224
  1271.0 79.0 %reduce-scatter.18.cloned.1.call-done = f32[512,1600]{0,1:T(8,128)} async-done(((f32[1024,1600]{0,1:T(8,128)}), f32[512,1600]{0,1:T(8,128)}) %reduce-scatter.18.cloned.1.call-update) | async-done | bytes 3276816 | tf_op jit(solution)/shard_map/reduce_scatter | solution.py:225
  1353.2 14.7 convolution_convert_fusion.2
  1368.0 19.1 convolution_convert_fusion.1
  1387.3 18.9 convolution_convert_fusion
  1408.8 19.6 fusion.85
  1434.1 163.7 %reduce-scatter.20.cloned.1.call-done = bf16[800,4800]{1,0:T(8,128)(2,1)} async-done(((bf16[1600,4800]{1,0:T(8,128)(2,1)}), bf16[800,4800]{1,0:T(8,128)(2,1)}) %reduce-scatter.20.cloned.1.call-update) | async-done | bytes 7680016 | tf_op jit(solution)/shard_map/reduce_scatter | solution.py:238
  1597.9 231.9 %reduce-scatter.26.cloned.1.call-done = bf16[800,6400]{1,0:T(8,128)(2,1)} async-done(((bf16[1600,6400]{1,0:T(8,128)(2,1)}), bf16[800,6400]{1,0:T(8,128)(2,1)}) %reduce-scatter.26.cloned.1.call-update) | async-done | bytes 10240016
  1829.8 15.7 copy.47
  1850.0 439.4 %all-reduce.29.cloned.1.call-done = bf16[6400,1600]{0,1:T(8,128)(2,1)} async-done(((bf16[6400,1600]{0,1:T(8,128)(2,1)}), bf16[6400,1600]{0,1:T(8,128)(2,1)}) %all-reduce.29.cloned.1.call-update) | async-done | bytes 20480016
  2289.4 8.4 constant_dynamic-slice_fusion.1
  2297.9 147.6 %fusion.4 = bf16[3200,112]{0,1:T(8,128)(2,1)} fusion(bf16[3200,1600]{0,1:T(8,128)(2,1)} %constant_dynamic-slice_fusion.1), kind=kCustom, calls=%all-reduce-scatter | all-reduce-scatter fusion | flops 5734401 | bytes 10957312
  2447.4 17.8 collective-permute-start
  2469.5 22.0 fusion.68
  2497.8 59.8 %all-reduce.21 = (f32[800]{0:T(1024)}, f32[800]{0:T(1024)}, f32[1600]{0:T(1024)}, f32[800]{0:T(1024)}, f32[800]{0:T(1024)}, /*index=5*/f32[800]{0:T(1024)}, f32[3200]{0:T(1024)}, f32[800]{0:T(1024)}) all-reduce(f32[800]{0:T(1024)S(1)} %dynamic-slice.9, f32[800]{0:T(1024)S(1)} %dynamic-slice.11, ...), channel_id=1, replica_groups=mesh['rep'=16,'fsdp'=2] {'rep'}, use_global_device_ids=true, to_apply=%region_19.20 | all-reduce | flops 9600 | bytes 76800 | tf_op jit(solution)/shard_map/psum | solution.py:266
  2557.6 11.3 concatenate.8
  2581.9 131.6 %reduce-scatter.24.cloned.1.call-done = bf16[400,800]{1,0:T(8,128)(2,1)} async-done(((bf16[6400,800]{1,0:T(8,128)(2,1)}), bf16[400,800]{1,0:T(8,128)(2,1)}) %reduce-scatter.24.cloned.1.call-update) | async-done | bytes 640016
  (477 shorter events, 446.7 us)
Async XLA Ops:
  7.3 15.0 copy-start
  7.3 190.4 %all-gather.8.cloned.1.call-start = ((), (), s32[]{:S(2)}) async-start(), calls=%async_computation.6 | async-start | bytes 23347200 | tf_op jit(solution)/shard_map/all_gather | solution.py:59
  8.0 254.9 %all-gather.10.cloned.1.call-start = ((), (), s32[]{:S(2)}) async-start(), calls=%async_computation.7 | async-start | bytes 4915200 | tf_op jit(solution)/shard_map/all_gather | solution.py:75
  22.3 190.7 %copy-start.19 = (f32[1600]{0:T(1024)}, f32[1600]{0:T(1024)S(1)}, u32[]{:S(2)}) copy-start(f32[1600]{0:T(1024)S(1)} %convert_element_type.140) | copy-start | bytes 19204
  22.3 190.7 %copy-start.10 = (f32[1600]{0:T(1024)}, f32[1600]{0:T(1024)S(1)}, u32[]{:S(2)}) copy-start(f32[1600]{0:T(1024)S(1)} %convert_element_type.139) | copy-start | bytes 19204
  22.6 190.4 %copy-start.12 = (f32[512]{0:T(512)}, f32[512]{0:T(512)S(1)}, u32[]{:S(2)}) copy-start(f32[512]{0:T(512)S(1)} %broadcast_multiply_fusion.1) | copy-start | bytes 6148
  23.7 189.3 %copy-start.16 = (f32[512]{0:T(512)}, f32[512]{0:T(512)S(1)}, u32[]{:S(2)}) copy-start(f32[512]{0:T(512)S(1)} %fusion.78) | copy-start | bytes 6148
  216.4 95.1 %all-gather.12.cloned.1.call-start = ((), (), s32[]{:S(2)}) async-start(), calls=%async_computation.8 | async-start | bytes 4915200 | tf_op jit(solution)/shard_map/all_gather | solution.py:76
  220.8 203.7 %all-gather.14.cloned.1.call-start = ((), (), s32[]{:S(2)}) async-start(), calls=%async_computation.9 | async-start | bytes 7987200 | tf_op jit(solution)/shard_map/all_gather | solution.py:61
  221.4 404.5 %all-gather.16.cloned.1.call-start = ((), (), s32[]{:S(2)}) async-start(), calls=%async_computation.10 | async-start | bytes 30720000 | tf_op jit(solution)/shard_map/all_gather | solution.py:110
  222.0 647.2 %all-gather.18.cloned.1.call-start = ((), (), s32[]{:S(2)}) async-start(), calls=%async_computation.11 | async-start | bytes 30720000 | tf_op jit(solution)/shard_map/all_gather | solution.py:112
  222.5 1045.0 %reduce-scatter.16.cloned.1.call-start = ((), (), s32[]{:S(2)}) async-start(), calls=%async_computation.12 | async-start | bytes 9830400 | tf_op jit(solution)/shard_map/reduce_scatter | solution.py:224
  647.1 252.0 %copy-start.3 = (f32[512,1600]{0,1:T(8,128)S(1)}, f32[512,1600]{0,1:T(8,128)}, u32[]{:S(2)}) copy-start(f32[512,1600]{0,1:T(8,128)} %copy-done.2) | copy-start | bytes 9830404
  899.1 21.4 copy-start.4
  924.7 7.3 copy-start.8
  1187.5 162.4 %reduce-scatter.18.cloned.1.call-start = ((), (), s32[]{:S(2)}) async-start(), calls=%async_computation.13 | async-start | bytes 9830400 | tf_op jit(solution)/shard_map/reduce_scatter | solution.py:225
  1188.3 245.8 %reduce-scatter.22.cloned.1.call-start = ((), (), s32[]{:S(2)}) async-start(), calls=%async_computation.15 | async-start | bytes 7987200 | tf_op jit(solution)/shard_map/reduce_scatter | solution.py:173
  1196.3 401.5 %reduce-scatter.20.cloned.1.call-start = ((), (), s32[]{:S(2)}) async-start(), calls=%async_computation.14 | async-start | bytes 23347200 | tf_op jit(solution)/shard_map/reduce_scatter | solution.py:238
  1270.9 82.2 %copy-start.11 = (f32[1600]{0:T(1024)S(1)}, f32[1600]{0:T(1024)}, u32[]{:S(2)}) copy-start(f32[1600]{0:T(1024)} %copy-done.10) | copy-start | bytes 19204
  1270.9 82.2 %copy-start.13 = (f32[512]{0:T(512)S(1)}, f32[512]{0:T(512)}, u32[]{:S(2)}) copy-start(f32[512]{0:T(512)} %copy-done.12) | copy-start | bytes 6148
  1271.0 82.2 %copy-start.17 = (f32[512]{0:T(512)S(1)}, f32[512]{0:T(512)}, u32[]{:S(2)}) copy-start(f32[512]{0:T(512)} %copy-done.16) | copy-start | bytes 6148
  1271.0 82.2 %copy-start.20 = (f32[1600]{0:T(1024)S(1)}, f32[1600]{0:T(1024)}, u32[]{:S(2)}) copy-start(f32[1600]{0:T(1024)} %copy-done.19) | copy-start | bytes 19204
  1367.9 461.8 %reduce-scatter.26.cloned.1.call-start = ((), (), s32[]{:S(2)}) async-start(), calls=%async_computation.18 | async-start | bytes 30720000
  1387.1 902.4 %all-reduce.29.cloned.1.call-start = ((), (), s32[]{:S(2)}) async-start(), calls=%async_computation.17 | async-start | bytes 40960000
  1406.2 1085.3 %all-reduce.31.cloned.1.call-start = ((), (), s32[]{:S(2)}) async-start(), calls=%async_computation.19 | async-start | bytes 188416
  1408.7 19.7 copy-start.15
  1408.8 19.7 copy-start.1
  1434.0 1143.1 %all-reduce.33.cloned.1.call-start = ((), (), s32[]{:S(2)}) async-start(), calls=%async_computation.20 | async-start | bytes 20889600
  1597.8 1115.7 %reduce-scatter.24.cloned.1.call-start = ((), (), s32[]{:S(2)}) async-start(), calls=%async_computation.16 | async-start | bytes 12185600
  2297.9 171.6 %copy-start.5 = (f32[512,1600]{0,1:T(8,128)S(1)}, f32[512,1600]{0,1:T(8,128)}, u32[]{:S(2)}) copy-start(f32[512,1600]{0,1:T(8,128)} %copy-done.2) | copy-start | bytes 9830404
  2447.4 110.2 %collective-permute-start = (bf16[3200,112]{0,1:T(8,128)(2,1)}, bf16[3200,112]{0,1:T(8,128)(2,1)}, u32[]{:S(2)}, u32[]{:S(2)}) collective-permute-start(bf16[3200,112]{0,1:T(8,128)(2,1)} %fusion.4), channel_id=1, source_target_pairs={{0,2},{2,4},{4,6},{6,8},{8,10},{10,12},{12,14},{14,16},{16,18},{18... | collective-permute-start | bytes 2150408
  2465.2 92.4 %collective-permute-start.1 = (bf16[3200,68]{0,1:T(8,128)(2,1)}, bf16[3200,68]{0,1:T(8,128)(2,1)}, u32[]{:S(2)}, u32[]{:S(2)}) collective-permute-start(bf16[3200,68]{0,1:T(8,128)(2,1)} %slice.26), channel_id=1, source_target_pairs={{0,4},{2,6},{4,8},{6,10},{8,12},{10,14},{12,16},{14,18},{16,20},{1... | collective-permute-start | bytes 1305608
  (17 other events, 42.6 us)
Sparse Core Ops, SparseCore 0:
  9.7 187.9 all-gather.7
  216.5 46.4 all-gather.9
  265.1 46.3 all-gather.11
  312.9 69.4 all-gather.13
  383.8 241.9 all-gather.15
  627.2 241.8 all-gather.17
  1187.6 79.8 reduce-scatter.15
  1270.0 79.8 reduce-scatter.17
  1352.2 66.5 reduce-scatter.21
  1421.1 176.6 reduce-scatter.19
  1600.1 229.6 reduce-scatter.25
  1832.1 457.3 all-reduce.28
  2293.3 23.4 all-reduce.30
  2320.4 256.5 all-reduce.32
  2581.4 131.9 reduce-scatter.23
where the time goes:
time: 2740 us; the launch traced here: 2720 us
  waiting for transfers between devices  1790 us (65%)
  matrix products  536 us (20%)
  blocking collectives  223 us (8%)
  local copies, waits for them, and re-layouts  82.5 us (3%)
  other arithmetic  47.4 us (2%)
    unnamed x22, waiting for transfers between devices  813 us
    all_gather x1, waiting for transfers between devices, local(): lax.all_gather(reduce_weight, 'fsdp', axis=0, tiled=True)  222 us
    all_gather x1, waiting for transfers between devices, local(): lax.all_gather(expand_weight, 'fsdp', axis=0, tiled=True)  193 us
    all_gather x1, waiting for transfers between devices, local(): lax.all_gather(input_weight, 'fsdp', axis=0, tiled=True)  174 us
    reduce_scatter x1, waiting for transfers between devices, local(): lax.psum_scatter(jnp.einsum('tr,te->re', normed_low, mixed_grad, preferre...  164 us
    unnamed x2, blocking collectives  158 us
    dot_general x50, matrix products, head_scores(): jnp.einsum('qd,kd->qk', query_one, key_one, preferred_element_type=floating)  107 us
    reduce_scatter x1, waiting for transfers between devices, local(): lax.psum_scatter(value_part, 'fsdp', scatter_dimension=0, tiled=True)  79 us
  transfers between devices with their start and end apart: 17, of which 12 were waited for; matrix products, arithmetic and copies ran while one was open for 17% of the time, Pallas kernels for 0%

commit v1 on v0

v1 whole, which is shorter than its diff:
```python
import functools

import jax
import jax.numpy as jnp
from jax import lax
from jax.experimental import pallas as pl
from jax.experimental.pallas import tpu as pltpu
from jax.sharding import PartitionSpec as P

HEADS = 25
HEAD_DIM = 64
LANES = 128
norm_eps = 1e-05
masked_score = -1e30
score_scale = HEAD_DIM ** (-0.5)
brain = jnp.bfloat16
floating = jnp.float32


def nt(a, b):
    return lax.dot_general(a, b, (((1,), (1,)), ((), ())), preferred_element_type=floating)


def nn(a, b):
    return lax.dot_general(a, b, (((1,), (0,)), ((), ())), preferred_element_type=floating)


def fill_bias(segc_ref, segr_ref, bias_ref, block):
    total = segr_ref.shape[1]
    for qi in range(total // block):
        rows = (qi + 1) * block
        seg_k = segc_ref[0:rows, :]
        seg_q = segr_ref[:, qi * block : (qi + 1) * block]
        pos_k = lax.broadcasted_iota(jnp.int32, (rows, block), 0)
        pos_q = lax.broadcasted_iota(jnp.int32, (rows, block), 1) + qi * block
        seen = (pos_k <= pos_q) & ((seg_k == 0) | (seg_k == seg_q))
        bias_ref[0:rows, qi * block : (qi + 1) * block] = jnp.where(seen, 0.0, masked_score)


def half_lanes(value, e):
    lane = lax.broadcasted_iota(jnp.int32, value.shape, 1)
    return jnp.where((lane // HEAD_DIM) == e, value, jnp.zeros_like(value))


def attend_kernel(meta, segc_ref, segr_ref, x_ref, o_ref, lse_ref, bias_ref, q_ref, k_ref, vt_ref, ot_ref, *, block, own):
    total = x_ref.shape[0]
    blocks = total // block
    me = meta[0]
    p = pl.program_id(0)

    @pl.when(p == 0)
    def _():
        fill_bias(segc_ref, segr_ref, bias_ref, block)

    def where_is(b):
        return pl.multiple_of(jnp.bitwise_xor(b, me * (own // block)) * block, block)

    for b in range(blocks):
        rows = pl.ds(where_is(b), block)
        q_ref[b * block : (b + 1) * block, :] = x_ref[rows, 0:LANES] * jnp.asarray(score_scale, brain)
        k_ref[b * block : (b + 1) * block, :] = x_ref[rows, LANES : 2 * LANES]
        vt_ref[:, b * block : (b + 1) * block] = x_ref[rows, 2 * LANES : 3 * LANES].T
    for e in range(2):
        valid = meta[1 + 2 * p + e] == 1
        feats = slice(e * HEAD_DIM, (e + 1) * HEAD_DIM)

        @pl.when(valid)
        def _():
            for qi in range(blocks):
                cols = slice(qi * block, (qi + 1) * block)
                keys = (qi + 1) * block
                query = half_lanes(q_ref[cols, :], e)
                scores = nt(k_ref[0:keys, :], query) + bias_ref[0:keys, cols]
                largest = jnp.max(scores, axis=0, keepdims=True)
                exponent = jnp.exp(scores - largest)
                denominator = jnp.sum(exponent, axis=0, keepdims=True)
                context = nn(vt_ref[feats, 0:keys], exponent.astype(brain)) / denominator
                ot_ref[feats, cols] = context
                lse_ref[0, e : e + 1, cols] = largest + jnp.log(denominator)

        @pl.when(jnp.logical_not(valid))
        def _():
            ot_ref[feats, :] = jnp.zeros((HEAD_DIM, total), floating)
            lse_ref[0, e : e + 1, :] = jnp.zeros((1, total), floating)

    for b in range(blocks):
        o_ref[pl.ds(where_is(b), block), :] = ot_ref[:, b * block : (b + 1) * block].T.astype(brain)


def attend_back_kernel(
    meta, segc_ref, segr_ref, x_ref, o_ref, do_ref, lse_ref, dx_ref,
    bias_ref, q_ref, k_ref, v_ref, d_ref, kt_ref, delta_ref, dqt_ref, dk_ref, dv_ref, *, block, own,
):
    total = x_ref.shape[0]
    blocks = total // block
    me = meta[0]
    p = pl.program_id(0)

    @pl.when(p == 0)
    def _():
        fill_bias(segc_ref, segr_ref, bias_ref, block)

    def where_is(b):
        return pl.multiple_of(jnp.bitwise_xor(b, me * (own // block)) * block, block)

    for b in range(blocks):
        rows = pl.ds(where_is(b), block)
        here = slice(b * block, (b + 1) * block)
        q_ref[here, :] = x_ref[rows, 0:LANES] * jnp.asarray(score_scale, brain)
        key = x_ref[rows, LANES : 2 * LANES]
        k_ref[here, :] = key
        kt_ref[:, here] = (key * jnp.asarray(score_scale, brain)).T
        v_ref[here, :] = x_ref[rows, 2 * LANES : 3 * LANES]
        grad = do_ref[rows, :]
        d_ref[here, :] = grad
        both = (grad.astype(floating) * o_ref[rows, :].astype(floating)).T
        delta_ref[0:1, here] = jnp.sum(both[0:HEAD_DIM, :], axis=0, keepdims=True)
        delta_ref[1:2, here] = jnp.sum(both[HEAD_DIM:, :], axis=0, keepdims=True)
    dk_ref[...] = jnp.zeros_like(dk_ref)
    dv_ref[...] = jnp.zeros_like(dv_ref)
    for e in range(2):
        valid = meta[1 + 2 * p + e] == 1
        feats = slice(e * HEAD_DIM, (e + 1) * HEAD_DIM)

        @pl.when(valid)
        def _():
            for qi in range(blocks):
                cols = slice(qi * block, (qi + 1) * block)
                keys = (qi + 1) * block
                query = half_lanes(q_ref[cols, :], e)
                grad = half_lanes(d_ref[cols, :], e)
                scores = nt(k_ref[0:keys, :], query) + bias_ref[0:keys, cols]
                prob = jnp.exp(scores - lse_ref[0, e : e + 1, cols])
                prob_grad = nt(v_ref[0:keys, :], grad)
                score_grad = (prob * (prob_grad - delta_ref[e : e + 1, cols])).astype(brain)
                dqt_ref[feats, cols] = nn(kt_ref[feats, 0:keys], score_grad)
                dv_ref[0:keys, :] += nn(prob.astype(brain), grad)
                dk_ref[0:keys, :] += nn(score_grad, query)

        @pl.when(jnp.logical_not(valid))
        def _():
            dqt_ref[feats, :] = jnp.zeros((HEAD_DIM, total), floating)

    for b in range(blocks):
        rows = pl.ds(where_is(b), block)
        here = slice(b * block, (b + 1) * block)
        dx_ref[rows, 0:LANES] = dqt_ref[:, here].T.astype(brain)
        dx_ref[rows, LANES : 2 * LANES] = dk_ref[here, :].astype(brain)
        dx_ref[rows, 2 * LANES : 3 * LANES] = dv_ref[here, :].astype(brain)


def attend(meta, segments, mixed, own):
    total, width = mixed.shape
    pairs = width // (3 * LANES)
    block = min(own, 256)
    fixed = lambda p, m: (0, 0)
    macs = total * total * LANES * pairs * 2
    return pl.pallas_call(
        functools.partial(attend_kernel, block=block, own=own),
        grid_spec=pltpu.PrefetchScalarGridSpec(
            num_scalar_prefetch=1,
            grid=(pairs,),
            in_specs=[
                pl.BlockSpec((total, 1), fixed),
                pl.BlockSpec((1, total), fixed),
                pl.BlockSpec((total, 3 * LANES), lambda p, m: (0, p)),
            ],
            out_specs=[
                pl.BlockSpec((total, LANES), lambda p, m: (0, p)),
                pl.BlockSpec((1, 8, total), lambda p, m: (p, 0, 0)),
            ],
            scratch_shapes=[
                pltpu.VMEM((total, total), floating),
                pltpu.VMEM((total, LANES), brain),
                pltpu.VMEM((total, LANES), brain),
                pltpu.VMEM((LANES, total), brain),
                pltpu.VMEM((LANES, total), floating),
            ],
        ),
        out_shape=[
            jax.ShapeDtypeStruct((total, pairs * LANES), brain),
            jax.ShapeDtypeStruct((pairs, 8, total), floating),
        ],
        compiler_params=pltpu.CompilerParams(vmem_limit_bytes=40 * 2**20),
        cost_estimate=pl.CostEstimate(
            flops=2 * macs, bytes_accessed=total * width * 3, transcendentals=total * total * pairs
        ),
        name="attend",
    )(meta, segments.reshape(total, 1), segments.reshape(1, total), mixed)


def attend_back(meta, segments, mixed, context, grad, log_total, own):
    total, width = mixed.shape
    pairs = width // (3 * LANES)
    block = min(own, 256)
    fixed = lambda p, m: (0, 0)
    macs = total * total * LANES * pairs * 5
    return pl.pallas_call(
        functools.partial(attend_back_kernel, block=block, own=own),
        grid_spec=pltpu.PrefetchScalarGridSpec(
            num_scalar_prefetch=1,
            grid=(pairs,),
            in_specs=[
                pl.BlockSpec((total, 1), fixed),
                pl.BlockSpec((1, total), fixed),
                pl.BlockSpec((total, 3 * LANES), lambda p, m: (0, p)),
                pl.BlockSpec((total, LANES), lambda p, m: (0, p)),
                pl.BlockSpec((total, LANES), lambda p, m: (0, p)),
                pl.BlockSpec((1, 8, total), lambda p, m: (p, 0, 0)),
            ],
            out_specs=pl.BlockSpec((total, 3 * LANES), lambda p, m: (0, p)),
            scratch_shapes=[
                pltpu.VMEM((total, total), floating),
                pltpu.VMEM((total, LANES), brain),
                pltpu.VMEM((total, LANES), brain),
                pltpu.VMEM((total, LANES), brain),
                pltpu.VMEM((total, LANES), brain),
                pltpu.VMEM((LANES, total), brain),
                pltpu.VMEM((8, total), floating),
                pltpu.VMEM((LANES, total), floating),
                pltpu.VMEM((total, LANES), floating),
                pltpu.VMEM((total, LANES), floating),
            ],
        ),
        out_shape=jax.ShapeDtypeStruct((total, width), brain),
        compiler_params=pltpu.CompilerParams(vmem_limit_bytes=40 * 2**20),
        cost_estimate=pl.CostEstimate(
            flops=2 * macs, bytes_accessed=total * width * 6, transcendentals=total * total * pairs
        ),
        name="attend_back",
    )(meta, segments.reshape(total, 1), segments.reshape(1, total), mixed, context, grad, log_total)


def stats(values):
    average = jnp.mean(values, axis=-1, keepdims=True)
    centered = values - average
    variance = jnp.mean(centered * centered, axis=-1, keepdims=True)
    return average, lax.rsqrt(variance + norm_eps)


def norm_back(values, average, inverse, gain, grad):
    unit = (values - average) * inverse
    scaled = grad * gain
    middle = jnp.mean(scaled, axis=-1, keepdims=True)
    along = jnp.mean(scaled * unit, axis=-1, keepdims=True)
    return inverse * (scaled - middle - unit * along), jnp.sum(grad * unit, axis=0), jnp.sum(grad, axis=0)


def tn(a, b):
    return lax.dot_general(a, b, (((0,), (0,)), ((), ())), preferred_element_type=floating)


def local(
    devices, reps,
    activations, segments, attend_gain, attend_shift, input_weight, input_bias, output_weight, output_bias,
    dense_gain, dense_shift, expand_weight, expand_bias, reduce_weight, reduce_bias, cotangent,
):
    me = lax.axis_index("fsdp")
    rep = lax.axis_index("rep")
    core = rep & 1
    tokens = activations[0].astype(floating)
    own, width = tokens.shape
    total = own * devices
    hidden = expand_weight.shape[1]
    hidden_own = hidden // devices
    all_pairs = -(-HEADS // 2)
    heads_own = -(-HEADS // devices)
    pairs = (heads_own + 1) // 2
    starts = [min(heads_own * f // 2, all_pairs - pairs) for f in range(devices)]
    start_of = lambda f: jnp.minimum(heads_own * f // 2, all_pairs - pairs)
    slot_heads = 2 * start_of(me) + jnp.arange(2 * pairs, dtype=jnp.int32)
    valid = (slot_heads >= heads_own * me) & (slot_heads < jnp.minimum(heads_own * (me + 1), HEADS))
    meta = jnp.concatenate([me[None].astype(jnp.int32), valid.astype(jnp.int32)])

    def fswap(value, d=1):
        return lax.ppermute(value, "fsdp", [(i, i ^ d) for i in range(devices)])

    def rswap(value, bit):
        return lax.ppermute(value, "rep", [(i, i ^ bit) for i in range(reps)])

    def gather_tokens(value):
        return jnp.concatenate([value] + [fswap(value, d) for d in range(1, devices)], axis=0)

    def in_order(parts):
        if devices == 2:
            return [jnp.where(me == f, parts[0], parts[1]) for f in range(2)]
        stacked = jnp.stack(parts)
        return [lax.dynamic_index_in_dim(stacked, me ^ f, 0, keepdims=False) for f in range(devices)]

    def fetch(weight, columns):
        rows = weight.shape[0]
        half = rows // 2
        mine = columns(weight, me)
        shape = (devices, 2, half) + mine.shape[1:]
        result = jnp.broadcast_to(mine.reshape((1, 2, half) + mine.shape[1:]), shape)
        part = lax.dynamic_slice_in_dim(weight, core * half, half, 0)
        zero = [0] * (mine.ndim - 1)
        for d in range(1, devices):
            first = fswap(columns(part, me ^ d), d)
            second = rswap(first, 1)
            result = lax.dynamic_update_slice(result, first[None, None], [me ^ d, core, 0] + zero)
            result = lax.dynamic_update_slice(result, second[None, None], [me ^ d, core ^ 1, 0] + zero)
        return result.reshape((devices * rows,) + mine.shape[1:])

    def pair_columns(weight, f):
        rows = weight.shape[0]
        padded = jnp.pad(weight.reshape(rows, 3, width), ((0, 0), (0, 0), (0, all_pairs * LANES - width)))
        padded = padded.reshape(rows, 3, all_pairs, LANES)
        taken = lax.dynamic_slice_in_dim(padded, start_of(f), pairs, 2)
        return taken.transpose(0, 2, 1, 3).reshape(rows, pairs * 3 * LANES)

    def hidden_columns(weight, f):
        return lax.dynamic_slice_in_dim(weight, f * hidden_own, hidden_own, 1)

    small = jnp.concatenate(
        [attend_gain, attend_shift, output_bias, dense_gain, dense_shift, reduce_bias, input_bias]
    )
    gathered = lax.all_gather(small, "fsdp", axis=0, tiled=False)
    piece = attend_gain.shape[0]
    full = [gathered[:, i * piece : (i + 1) * piece].reshape(-1).astype(floating) for i in range(6)]
    first_gain, first_shift, after_bias, second_gain, second_shift, last_bias = full
    mixing_bias = gathered[:, 6 * piece :].reshape(-1)
    three_bias = jnp.concatenate([mixing_bias[:width], jnp.zeros((width,), brain), mixing_bias[width:]])
    own_bias = pair_columns(three_bias[None], me).astype(floating)

    average, inverse = stats(tokens)
    normed = ((tokens - average) * inverse * first_gain + first_shift).astype(brain)
    input_own = fetch(input_weight, pair_columns)
    normed_all = gather_tokens(normed)
    mixed = (nn(normed_all, input_own) + own_bias).astype(brain)
    context_all, log_total = attend(meta, segments[0], mixed, own)

    def place(parts):
        ordered = in_order(parts)
        result = 0
        for f in range(devices):
            before = starts[f] * LANES
            after = all_pairs * LANES - before - pairs * LANES
            result = result + jnp.pad(ordered[f], ((0, 0), (before, after)))
        return result[:, :width]

    context = place(
        [context_all[:own]] + [fswap(context_all[d * own : (d + 1) * own], d) for d in range(1, devices)]
    )
    output_full = fetch(output_weight, lambda w, f: w)
    middle = tokens + (nn(context, output_full) + after_bias)

    average_2, inverse_2 = stats(middle)
    dense = ((middle - average_2) * inverse_2 * second_gain + second_shift).astype(brain)
    expand_own = fetch(expand_weight, hidden_columns)
    incoming_low = cotangent[0]
    incoming = incoming_low.astype(floating)
    incoming_all = gather_tokens(incoming_low)
    activated_grad = nt(incoming_all, reduce_weight).astype(brain)
    dense_all = gather_tokens(dense)
    expanded = nn(dense_all, expand_own) + expand_bias.astype(floating)
    activated, gelu_pull = jax.vjp(lambda v: jax.nn.gelu(v, approximate=True), expanded)
    activated = activated.astype(brain)
    expanded_grad = gelu_pull(activated_grad.astype(floating))[0].astype(brain)

    def scatter_tokens(left, right, product):
        result = product(left[:own], right)
        for d in range(1, devices):
            sent = product(left[d * own : (d + 1) * own], right).astype(brain)
            result = result + fswap(sent, d).astype(floating)
        return result

    dense_bar = scatter_tokens(expanded_grad, expand_own, nt)
    outputs = (middle + (scatter_tokens(activated, reduce_weight, nn) + last_bias)).astype(brain)
    norm_grad, dense_gain_part, dense_shift_part = norm_back(middle, average_2, inverse_2, second_gain, dense_bar)
    middle_grad = incoming + norm_grad
    attended_low = middle_grad.astype(brain)

    def halve(value, axis, bit):
        mine = (rep // bit) & 1
        sent = rswap(lax.dynamic_index_in_dim(value, mine ^ 1, axis, keepdims=False), bit)
        kept = lax.dynamic_index_in_dim(value, mine, axis, keepdims=False)
        return (kept.astype(floating) + sent.astype(floating)).astype(brain)

    def bits_of(count):
        return [1 << i for i in range(count.bit_length() - 1)]

    def halve_all(value, bits):
        low = bits[0]
        for bit in bits:
            value = value.reshape((value.shape[0] // 2, 2) + value.shape[1:])
            value = halve(value, 1, bit)
        return value[0]

    def columns_of(value, d):
        part = value.shape[-1] // devices
        return lax.dynamic_slice_in_dim(value, (me ^ d) * part, part, value.ndim - 1)

    reduce_grad = tn(incoming_all, activated).astype(brain).reshape(reps, width // reps, hidden_own)
    reduce_grad = halve_all(reduce_grad, bits_of(reps)).astype(floating).T

    local_blocks = reps // devices
    expand_grad = tn(expanded_grad, dense_all).astype(brain).reshape(local_blocks, hidden // reps, width)
    expand_grad = halve_all(expand_grad, bits_of(local_blocks))
    parts = [columns_of(expand_grad, 0)] + [fswap(columns_of(expand_grad, d), d) for d in range(1, devices)]
    expand_grad = jnp.stack(in_order(parts))
    expand_grad = halve_all(expand_grad, [bit * local_blocks for bit in bits_of(devices)]).astype(floating).T

    context_bar = nt(attended_low, output_full).astype(brain)
    context_bar_pad = jnp.pad(context_bar, ((0, 0), (0, all_pairs * LANES - width)))
    take_pairs = lambda f: lax.dynamic_slice_in_dim(context_bar_pad, start_of(f) * LANES, pairs * LANES, 1)
    context_bar_all = jnp.concatenate(
        [take_pairs(me)] + [fswap(take_pairs(me ^ d), d) for d in range(1, devices)], axis=0
    )
    output_grad = tn(attended_low, context).astype(brain).reshape(reps, width // reps, width)
    output_grad = halve_all(output_grad, bits_of(reps))
    output_sum = columns_of(output_grad, 0).astype(floating)
    for d in range(1, devices):
        output_sum = output_sum + fswap(columns_of(output_grad, d), d).astype(floating)
    output_grad = output_sum.T

    mixed_bar = attend_back(meta, segments[0], mixed, context_all, context_bar_all, log_total, own)
    normed_bar = scatter_tokens(mixed_bar, input_own, nt)
    token_grad, attend_gain_part, attend_shift_part = norm_back(tokens, average, inverse, first_gain, normed_bar)
    input_grads = (middle_grad + token_grad).astype(brain)

    quarter = width // devices // 2
    normed_quarters = normed_all.reshape(total, devices, 2, quarter)
    take = lambda c: lax.dynamic_index_in_dim(normed_quarters, c, 2, keepdims=False).reshape(total, devices * quarter)
    sent = rswap(tn(take(core ^ 1), mixed_bar).astype(brain), 1)
    input_grad = (tn(take(core), mixed_bar) + sent.astype(floating)).astype(brain)
    input_grad = input_grad.reshape(devices, quarter, pairs * 3 * LANES)
    pick = lambda d: lax.dynamic_index_in_dim(input_grad, me ^ d, 0, keepdims=False)
    ordered = in_order([pick(0)] + [fswap(pick(d), d) for d in range(1, devices)])
    columns = 0
    for f in range(devices):
        shaped = ordered[f].reshape(quarter, pairs, 3, LANES)
        columns = columns + jnp.pad(shaped, ((0, 0), (starts[f], all_pairs - pairs - starts[f]), (0, 0), (0, 0)))
    columns = columns.transpose(0, 2, 1, 3).reshape(quarter, 3, all_pairs * LANES)[:, :, :width]
    columns = columns.reshape(quarter, reps // 2, 2 * 3 * width // reps).transpose(1, 0, 2)
    columns = halve_all(columns, [2 * bit for bit in bits_of(reps // 2)])
    columns = columns.reshape(quarter, 2, 3 * width // reps)
    kept = lax.dynamic_index_in_dim(columns, core, 1, keepdims=False)
    came = rswap(lax.dynamic_index_in_dim(columns, core ^ 1, 1, keepdims=False), 1)
    input_grad = jnp.concatenate([jnp.where(core == 0, kept, came), jnp.where(core == 0, came, kept)], axis=0)
    input_grad = input_grad.astype(floating)

    sums = jnp.sum(mixed_bar.astype(floating), axis=0).reshape(pairs, 3, LANES)
    bias_full = lax.dynamic_update_slice(jnp.zeros((all_pairs, 3, LANES), floating), sums, [start_of(me), 0, 0])
    bias_full = bias_full.transpose(1, 0, 2).reshape(3, all_pairs * LANES)[:, :width]
    expand_sum = lax.dynamic_update_slice(
        jnp.zeros((hidden,), floating), jnp.sum(expanded_grad.astype(floating), axis=0), [me * hidden_own]
    )
    vectors = [
        attend_gain_part, attend_shift_part, bias_full[0], bias_full[2],
        jnp.sum(attended_low.astype(floating), axis=0), dense_gain_part, dense_shift_part,
        jnp.sum(incoming, axis=0), expand_sum,
    ]
    flat = lax.psum(jnp.concatenate(vectors), ("rep", "fsdp"))

    def share(start, length):
        part = length // devices
        return lax.dynamic_slice_in_dim(flat, start + me * part, part, 0)

    w = width
    return (
        outputs[None],
        input_grads[None],
        share(0, w),
        share(w, w),
        input_grad,
        share(2 * w, 2 * w),
        output_grad,
        share(4 * w, w),
        share(5 * w, w),
        share(6 * w, w),
        expand_grad,
        share(8 * w, hidden),
        reduce_grad,
        share(7 * w, w),
    )


def solution(mesh):
    row, matrix = P("fsdp"), P("fsdp", None)
    tokens = P("rep", "fsdp", None)
    in_specs = (
        tokens, P("rep", None), row, row, matrix, row, matrix, row, row, row, matrix, row, matrix, row, tokens,
    )
    split = P("fsdp", "rep")
    out_specs = (tokens, tokens, row, row, split, row, split, row, row, row, split, row, split, row)
    return jax.shard_map(
        functools.partial(local, mesh.shape["fsdp"], mesh.shape["rep"]),
        mesh=mesh, in_specs=in_specs, out_specs=out_specs, check_vma=False,
    )
```

time: 2740 us -> 1030 us (0.38)
  waiting for transfers between devices: 1790 us -> 313 us
  matrix products: 536 us -> 206 us
  local copies, waits for them, and re-layouts: 82.5 us -> 271 us
  blocking collectives: 223 us -> 48.8 us
  Pallas kernels: 0 us -> 69.2 us
    unnamed x22 -> x1, waiting for transfers between devices: 813 us -> 0.02 us
    all_gather x6 -> x0, waiting for transfers between devices: 663 us -> none  [the longest x1 222 us: local(): lax.all_gather(reduce_weight, 'fsdp', axis=0, tiled=True)]
    dot_general x187 -> x16, matrix products: 536 us -> 206 us  [the longest x6 83.2 us: nt(): lax.dot_general(a, b, (((1,), (1,)), ((), ())), preferred_element_type=fl...]
    reduce_scatter x4 -> x0, waiting for transfers between devices: 314 us -> none  [the longest x1 164 us: local(): lax.psum_scatter(jnp.einsum('tr,te->re', normed_low, mixed_grad, preferre...]
    ppermute x0 -> x34, waiting for transfers between devices: none -> 204 us  [the longest x20 129 us: rswap(): return lax.ppermute(value, 'rep', [(i, i ^ bit) for i in range(reps)])]
    unnamed x2 -> x0, blocking collectives: 158 us -> none
    psum x0 -> x1, waiting for transfers between devices: none -> 109 us  [local(): flat = lax.psum(jnp.concatenate(vectors), ('rep', 'fsdp'))]
    pallas_call x0 -> x2, Pallas kernels: none -> 69.2 us  [the longest x1 37.8 us: attend_back(): pl.pallas_call(functools.partial(attend_back_kernel, block=block, own=own...]
  transfers between devices with their start and end apart: 17 -> 35, of which waited for: 12 -> 13; matrix products, arithmetic and copies ran while one was open for 17% -> 48% of each run, Pallas kernels for 0% -> 7%
where the time goes in v1:
time: 1030 us; the launch traced here: 1020 us
  waiting for transfers between devices  313 us (30%)
  local copies, waits for them, and re-layouts  271 us (26%)
  matrix products  206 us (20%)
  Pallas kernels  69.2 us (7%)
  other arithmetic  64.4 us (6%)
  blocking collectives  48.8 us (5%)
  starting transfers between devices  31.5 us (3%)
  between operations  15.7 us (2%)
    ppermute x20, waiting for transfers between devices, rswap(): return lax.ppermute(value, 'rep', [(i, i ^ bit) for i in range(reps)])  129 us
    psum x1, waiting for transfers between devices, local(): flat = lax.psum(jnp.concatenate(vectors), ('rep', 'fsdp'))  109 us
    dot_general x6, matrix products, nt(): lax.dot_general(a, b, (((1,), (1,)), ((), ())), preferred_element_type=fl...  83.2 us
    ppermute x14, waiting for transfers between devices, fswap(): return lax.ppermute(value, 'fsdp', [(i, i ^ d) for i in range(devices)])  74.4 us
    dot_general x5, matrix products, nn(): lax.dot_general(a, b, (((1,), (0,)), ((), ())), preferred_element_type=fl...  64.8 us
    dot_general x5, matrix products, tn(): lax.dot_general(a, b, (((0,), (0,)), ((), ())), preferred_element_type=fl...  57.9 us
    all_gather x1, blocking collectives, local(): gathered = lax.all_gather(small, 'fsdp', axis=0, tiled=False)  48.8 us
    pallas_call x1, Pallas kernels, attend_back(): pl.pallas_call(functools.partial(attend_back_kernel, block=block, own=own...  37.8 us
  transfers between devices with their start and end apart: 35, of which 13 were waited for; matrix products, arithmetic and copies ran while one was open for 48% of the time, Pallas kernels for 7%

profile of v1, /device:TPU:0, one launch (start us, length us, event | category | flops | bytes accessed | tf_op | source)
XLA Modules:
  0.0 1020.0 jit_solution(1988881568754276479)
XLA Ops:
  17.3 11.4 %reshape.283 = bf16[400,3,1600]{2,1,0:T(4,128)(2,1)} reshape(bf16[400,4800]{1,0:T(8,128)(2,1)} %constant_dynamic-slice_fusion.17) | data formatting | bytes 7680000 | tf_op jit(solution)/shard_map/reshape | solution.py:307
  35.7 12.4 %reshape.331 = bf16[400,3,13,128]{3,2,1,0:T(8,128)(2,1)} reshape(bf16[400,3,1664]{2,1,0:T(4,128)(2,1)} %pad.33) | data formatting | bytes 7987200 | tf_op jit(solution)/shard_map/reshape | solution.py:308
  60.9 48.8 %all-gather.1 = bf16[2,1,6400]{2,1,0:T(2,128)(2,1)S(1)} all-gather(bf16[1,1,6400]{2,1,0:T(2,128)(2,1)S(1)} %reshape.328), channel_id=2, replica_groups=mesh['rep'=16,'fsdp'=2] {'fsdp'}, dimensions={0}, use_global_device_ids=true | all-gather | bytes 38400 | tf_op jit(solution)/shard_map/all_gather | solution.py:318
  122.6 12.1 %copy.109 = bf16[800,4800]{0,1:T(8,128)(2,1)} copy(bf16[800,4800]{1,0:T(8,128)(2,1)} %param.19) | data formatting | bytes 15360000 | tf_op args[4]
  147.9 12.5 %copy.110 = bf16[800,7,3,128]{3,2,1,0:T(4,128)(2,1)} copy(bf16[800,7,3,128]{0,3,1,2:T(8,128)(2,1)} %dynamic-slice_bitcast_fusion.1) | data formatting | bytes 8601600 | tf_op jit(solution)/shard_map/transpose | solution.py:310
  160.4 11.7 %broadcast_in_dim.37 = bf16[2,400,2688]{2,1,0:T(8,128)(2,1)} reshape(bf16[800,7,3,128]{3,2,1,0:T(4,128)(2,1)} %copy.110) | data formatting | bytes 8601600 | tf_op jit(solution)/shard_map/broadcast_in_dim | solution.py:295
  196.6 14.8 %add_convert_fusion.x_ref = bf16[1024,2688]{1,0:T(8,128)(2,1)S(1)} fusion(bf16[1600,2688]{1,0:T(8,128)(2,1)} %bitcast.249, f32[2688]{0:T(1024)S(1)} %reshape.309, bf16[512,1600]{0,1:T(8,128)(2,1)} %collective-permute-done, bf16[512,1600]{0,1:T(8,128)(2,1)} %fusion.25), kind=kOutput, calls=%fused_computation.19 | convolution fusion | flops 8820097024 | bytes 17394176 | tf_op jit(solution)/shard_map/dot_general | solution.py:25
  211.4 31.4 %attend.1 = (bf16[1024,896]{1,0:T(8,128)(2,1)S(1)}, f32[7,8,1024]{2,1,0:T(8,128)S(1)}) custom-call(s32[15]{0:T(128)S(1)} %pad_add_fusion.3.meta, s32[1024,1]{1,0:T(8,128)S(1)} %copy.113.segc_ref, s32[1,1024]{1,0:T(1,128)S(1)} %copy-done.4, bf16[1024,2688]{1,0:T(8,128)(2,1)S(1)} %add_convert_fusion.x_ref), custom_call_target="tpu_custom_call" | custom-call | flops 3758096384 | bytes 8257536 | tf_op jit(solution)/shard_map/attend/pallas_call | solution.py:158
  248.6 16.6 %collective-permute-done.3 = bf16[512,896]{1,0:T(8,128)(2,1)S(1)} collective-permute-done((bf16[512,896]{1,0:T(8,128)(2,1)S(1)}, bf16[512,896]{1,0:T(8,128)(2,1)S(1)}, u32[]{:S(2)}, u32[]{:S(2)}) %collective-permute-start.3) | collective-permute-done | bytes 917536 | tf_op jit(solution)/shard_map/ppermute | solution.py:276
  288.5 23.1 %collective-permute-done.6 = bf16[512,1600]{0,1:T(8,128)(2,1)} collective-permute-done((bf16[512,1600]{0,1:T(8,128)(2,1)}, bf16[512,1600]{0,1:T(8,128)(2,1)}, u32[]{:S(2)}, u32[]{:S(2)}) %collective-permute-start.6) | collective-permute-done | bytes 1638432 | tf_op jit(solution)/shard_map/ppermute | solution.py:276
  311.6 24.5 %multiply_convert_fusion = (bf16[1024,3200]{1,0:T(8,128)(2,1)}, f32[1024,3200]{1,0:T(8,128)}) fusion(f32[3200]{0:T(1024)S(1)} %convert_element_type.397, bf16[1600,3200]{1,0:T(8,128)(2,1)} %bitcast.246, bf16[512,1600]{0,1:T(8,128)(2,1)} %collective-permute-done.6, bf16[512,1600]{0,1:T(8,128)(2,1)} %add_convert_fusion.3), kind=kOutput, calls=%fused_computation.17 | convolution fusion | flops 10525081600 | bytes 33190400 | tf_op jit(solution)/shard_map/dot_general | solution.py:25
  336.1 29.8 %convert_reduce_fusion = (f32[3200]{0:T(1024)S(1)}, bf16[1024,3200]{1,0:T(8,128)(2,1)}) fusion(f32[1024,3200]{1,0:T(8,128)} %get-tuple-element.122, f32[3200]{0:T(1024)S(1)} %convert_element_type.397, bf16[3200,1600]{0,1:T(8,128)(2,1)} %param.27, bf16[512,1600]{0,1:T(8,128)(2,1)} %collective-permute-done.10, bf16[512,1600]{0,1:T(8,128)(2,1)} %bitcast.21), kind=kOutput, calls=%fused_computation.16 | convolution fusion | flops 10574230528 | bytes 33203200 | tf_op jit(solution)/shard_map/dot_general | solution.py:21
  365.9 11.6 %fusion.46 = bf16[512,1600]{0,1:T(8,128)(2,1)} fusion(bf16[1600,3200]{1,0:T(8,128)(2,1)} %bitcast.247, bf16[1024,3200]{1,0:T(8,128)(2,1)} %get-tuple-element.125), kind=kOutput, calls=%fused_computation.82 | convolution fusion | flops 5243699200 | bytes 15155200 | tf_op jit(solution)/shard_map/dot_general | solution.py:21
  378.0 9.4 fusion.43
  388.8 15.1 %convolution_convert_fusion = bf16[3200,1600]{0,1:T(8,128)(2,1)} fusion(bf16[1024,3200]{1,0:T(8,128)(2,1)S(1)} %bitcast.268, bf16[512,1600]{0,1:T(8,128)(2,1)} %collective-permute-done.6, bf16[512,1600]{0,1:T(8,128)(2,1)} %add_convert_fusion.3), kind=kOutput, calls=%fused_computation.4 | convolution fusion | flops 10497433600 | bytes 20070400 | tf_op jit(solution)/shard_map/dot_general | solution.py:250
  403.9 16.1 %copy.127 = bf16[3200,1600]{1,0:T(8,128)(2,1)} copy(bf16[3200,1600]{0,1:T(8,128)(2,1)} %convolution_convert_fusion) | data formatting | bytes 20480000 | tf_op jit(solution)/shard_map/convert_element_type | solution.py:398
  425.4 17.2 %convolution_convert_fusion.1 = bf16[1600,3200]{1,0:T(8,128)(2,1)} fusion(bf16[1024,3200]{1,0:T(8,128)(2,1)} %get-tuple-element.121, bf16[512,1600]{0,1:T(8,128)(2,1)} %collective-permute-done.10, bf16[512,1600]{0,1:T(8,128)(2,1)} %bitcast.21), kind=kOutput, calls=%fused_computation.5 | convolution fusion | flops 10497433600 | bytes 20070400 | tf_op jit(solution)/shard_map/dot_general | solution.py:250
  442.6 10.7 %reshape_reshape.12 = bf16[8,2,100,3200]{3,2,1,0:T(8,128)(2,1)} reshape(bf16[1600,3200]{1,0:T(8,128)(2,1)} %convolution_convert_fusion.1) | data formatting | bytes 20480000 | tf_op jit(solution)/shard_map/reshape;reshape | solution.py:386
  453.3 9.5 fusion.39
  462.9 14.5 %multiply_reduce_fusion = (f32[1600]{0:T(1024)S(1)}, f32[512]{0:T(512)S(1)}, f32[512]{0:T(512)S(1)}, f32[1600]{0:T(1024)S(1)}, f32[512,1600]{0,1:T(8,128)S(1)}) fusion(f32[512,1600]{0,1:T(8,128)S(1)} %copy-done.9, f32[512]{0:T(512)S(1)} %copy-done.42, f32[512]{0:T(512)S(1)} %copy-done.37, f32[1600]{0:T(1024)S(1)} %copy-done.33, ...), kind=kOutput, calls=%fused_computation.72 | convolution fusion | flops 5251887104 | bytes 21736192 | tf_op jit(solution)/shard_map/dot_general | solution.py:21
  521.8 37.8 %attend_back.1 = bf16[1024,2688]{1,0:T(8,128)(2,1)S(1)} custom-call(s32[15]{0:T(128)S(1)} %copy-done.6, s32[1024,1]{1,0:T(8,128)S(1)} %copy.113.segc_ref, s32[1,1024]{1,0:T(1,128)S(1)} %copy-done.4, bf16[1024,2688]{1,0:T(8,128)(2,1)} %copy-done.7, bf16[1024,896]{1,0:T(8,128)(2,1)S(1)} %get-tuple-element.16.o_ref, ...), custom_call_target="tpu_custom_call" | custom-call | flops 9395240960 | bytes 16515072 | tf_op jit(solution)/shard_map/attend_back/pallas_call | solution.py:198
  559.7 11.6 %convolution_convert_fusion.6 = bf16[512,1600]{0,1:T(8,128)(2,1)} fusion(bf16[1600,2688]{1,0:T(8,128)(2,1)} %bitcast.250, bf16[1024,2688]{1,0:T(8,128)(2,1)S(1)} %attend_back.1), kind=kOutput, calls=%fused_computation.84 | convolution fusion | flops 4404838400 | bytes 12992512 | tf_op jit(solution)/shard_map/dot_general | solution.py:21
  574.3 10.1 convolution_convert_fusion.4
  585.0 24.2 %collective-permute-done.13 = bf16[512,1600]{0,1:T(8,128)(2,1)} collective-permute-done((bf16[512,1600]{0,1:T(8,128)(2,1)}, bf16[512,1600]{0,1:T(8,128)(2,1)}, u32[]{:S(2)}, u32[]{:S(2)}) %collective-permute-start.13) | collective-permute-done | bytes 1638432 | tf_op jit(solution)/shard_map/ppermute | solution.py:276
  629.2 109.2 %all-reduce.10.cloned.1.call-done = f32[19200]{0:T(1024)} async-done(((f32[19200]{0:T(1024)}), f32[19200]{0:T(1024)}) %all-reduce.10.cloned.1.call-update) | async-done | bytes 76816 | tf_op jit(solution)/shard_map/psum | solution.py:454
  786.4 10.3 %collective-permute-done.23 = bf16[1,100,1600]{2,1,0:T(8,128)(2,1)S(1)} collective-permute-done((bf16[1,100,1600]{2,1,0:T(8,128)(2,1)S(1)}, bf16[1,100,1600]{2,1,0:T(8,128)(2,1)S(1)}, u32[]{:S(2)}, u32[]{:S(2)}) %collective-permute-start.23) | collective-permute-done | bytes 320032 | tf_op jit(solution)/shard_map/ppermute | solution.py:279
  798.1 12.4 %collective-permute-done.26 = bf16[2,400,1600]{2,1,0:T(8,128)(2,1)} collective-permute-done((bf16[2,400,1600]{2,1,0:T(8,128)(2,1)}, bf16[2,400,1600]{2,1,0:T(8,128)(2,1)}, u32[]{:S(2)}, u32[]{:S(2)}) %collective-permute-start.26) | collective-permute-done | bytes 2560032 | tf_op jit(solution)/shard_map/ppermute | solution.py:279
  818.8 10.0 collective-permute-done.15
  893.7 26.5 %collective-permute-done.16 = bf16[4,400,600]{2,1,0:T(8,128)(2,1)} collective-permute-done((bf16[4,400,600]{2,1,0:T(8,128)(2,1)}, bf16[4,400,600]{2,1,0:T(8,128)(2,1)}, u32[]{:S(2)}, u32[]{:S(2)}) %collective-permute-start.16) | collective-permute-done | bytes 1920032 | tf_op jit(solution)/shard_map/ppermute | solution.py:279
  930.7 31.5 %collective-permute-done.17 = bf16[2,400,600]{2,1,0:T(8,128)(2,1)S(1)} collective-permute-done((bf16[2,400,600]{2,1,0:T(8,128)(2,1)S(1)}, bf16[2,400,600]{2,1,0:T(8,128)(2,1)S(1)}, u32[]{:S(2)}, u32[]{:S(2)}) %collective-permute-start.17) | collective-permute-done | bytes 960032 | tf_op jit(solution)/shard_map/ppermute | solution.py:279
  962.6 21.7 %collective-permute-done.33 = bf16[1,100,3200]{2,1,0:T(8,128)(2,1)S(1)} collective-permute-done((bf16[1,100,3200]{2,1,0:T(8,128)(2,1)S(1)}, bf16[1,100,3200]{2,1,0:T(8,128)(2,1)S(1)}, u32[]{:S(2)}, u32[]{:S(2)}) %collective-permute-start.33) | collective-permute-done | bytes 640032 | tf_op jit(solution)/shard_map/ppermute | solution.py:279
  985.5 18.4 %collective-permute-done.18 = bf16[1,400,600]{2,1,0:T(8,128)(2,1)S(1)} collective-permute-done((bf16[1,400,600]{2,1,0:T(8,128)(2,1)S(1)}, bf16[1,400,600]{2,1,0:T(8,128)(2,1)S(1)}, u32[]{:S(2)}, u32[]{:S(2)}) %collective-permute-start.18) | collective-permute-done | bytes 480032 | tf_op jit(solution)/shard_map/ppermute | solution.py:279
  (325 shorter events, 327.5 us)
Async XLA Ops:
  7.2 731.2 %all-reduce.10.cloned.1.call-start = ((), (), s32[]{:S(2)}) async-start(), calls=%async_computation | async-start | bytes 155648 | tf_op jit(solution)/shard_map/psum | solution.py:454
  10.1 168.4 %collective-permute-start.4 = (bf16[400,1600]{1,0:T(8,128)(2,1)}, bf16[400,1600]{1,0:T(8,128)(2,1)}, u32[]{:S(2)}, u32[]{:S(2)}) collective-permute-start(bf16[400,1600]{1,0:T(8,128)(2,1)} %constant_dynamic-slice_fusion.15), channel_id=1, source_target_pairs={{0,1},{1,0},{2,3},{3,2},{4,5},{5,4},{6,7},{7,6},{8,9},{9,8},{10,11... | collective-permute-start | bytes 3840008 | tf_op jit(solution)/shard_map/ppermute | solution.py:276
  60.8 112.6 %collective-permute-start.1 = (bf16[400,2688]{1,0:T(8,128)(2,1)}, bf16[400,2688]{1,0:T(8,128)(2,1)}, u32[]{:S(2)}, u32[]{:S(2)}) collective-permute-start(bf16[400,2688]{1,0:T(8,128)(2,1)} %reshape.285), channel_id=1, source_target_pairs={{0,1},{1,0},{2,3},{3,2},{4,5},{5,4},{6,7},{7,6},{8,9},{9,8},{10,11... | collective-permute-start | bytes 6451208 | tf_op jit(solution)/shard_map/ppermute | solution.py:276
  115.7 80.8 %collective-permute-start = (bf16[512,1600]{0,1:T(8,128)(2,1)}, bf16[512,1600]{0,1:T(8,128)(2,1)}, u32[]{:S(2)}, u32[]{:S(2)}) collective-permute-start(bf16[512,1600]{0,1:T(8,128)(2,1)} %fusion.25), channel_id=1, source_target_pairs={{0,1},{1,0},{2,3},{3,2},{4,5},{5,4},{6,7},{7,6},{8,9},{9,8},{10,11... | collective-permute-start | bytes 4915208 | tf_op jit(solution)/shard_map/ppermute | solution.py:276
  120.6 126.8 %collective-permute-start.7 = (bf16[400,3200]{1,0:T(8,128)(2,1)}, bf16[400,3200]{1,0:T(8,128)(2,1)}, u32[]{:S(2)}, u32[]{:S(2)}) collective-permute-start(bf16[400,3200]{1,0:T(8,128)(2,1)} %dynamic_slice.182), channel_id=1, source_target_pairs={{0,1},{1,0},{2,3},{3,2},{4,5},{5,4},{6,7},{7,6},{8,9},{9,8},{10,11... | collective-permute-start | bytes 7680008 | tf_op jit(solution)/shard_map/ppermute | solution.py:276
  122.4 213.7 %collective-permute-start.10 = (bf16[512,1600]{0,1:T(8,128)(2,1)}, bf16[512,1600]{0,1:T(8,128)(2,1)}, u32[]{:S(2)}, u32[]{:S(2)}) collective-permute-start(bf16[512,1600]{0,1:T(8,128)(2,1)} %bitcast.21), channel_id=1, source_target_pairs={{0,1},{1,0},{2,3},{3,2},{4,5},{5,4},{6,7},{7,6},{8,9},{9,8},{10,11... | collective-permute-start | bytes 4915208 | tf_op jit(solution)/shard_map/ppermute | solution.py:276
  173.3 20.2 %collective-permute-start.2 = (bf16[400,2688]{1,0:T(8,128)(2,1)}, bf16[400,2688]{1,0:T(8,128)(2,1)}, u32[]{:S(2)}, u32[]{:S(2)}) collective-permute-start(bf16[400,2688]{1,0:T(8,128)(2,1)} %collective-permute-done.1), channel_id=1, source_target_pairs={{0,2},{2,0},{4,6},{6,4},{8,10},{10,8},{12,14},{14,12},{16,18},{18,... | collective-permute-start | bytes 6451208 | tf_op jit(solution)/shard_map/ppermute | solution.py:279
  178.5 68.8 %collective-permute-start.5 = (bf16[400,1600]{1,0:T(8,128)(2,1)}, bf16[400,1600]{1,0:T(8,128)(2,1)S(1)}, u32[]{:S(2)}, u32[]{:S(2)}) collective-permute-start(bf16[400,1600]{1,0:T(8,128)(2,1)} %collective-permute-done.4), channel_id=1, source_target_pairs={{0,2},{2,0},{4,6},{6,4},{8,10},{10,8},{12,14},{14,12},{16,18},{18,... | collective-permute-start | bytes 3840008 | tf_op jit(solution)/shard_map/ppermute | solution.py:279
  242.9 22.3 %collective-permute-start.3 = (bf16[512,896]{1,0:T(8,128)(2,1)S(1)}, bf16[512,896]{1,0:T(8,128)(2,1)S(1)}, u32[]{:S(2)}, u32[]{:S(2)}) collective-permute-start(bf16[512,896]{1,0:T(8,128)(2,1)S(1)} %slice.79), channel_id=1, source_target_pairs={{0,1},{1,0},{2,3},{3,2},{4,5},{5,4},{6,7},{7,6},{8,9},{9,8},{10,11... | collective-permute-start | bytes 2752520 | tf_op jit(solution)/shard_map/ppermute | solution.py:276
  247.4 37.8 %collective-permute-start.8 = (bf16[400,3200]{1,0:T(8,128)(2,1)}, bf16[400,3200]{1,0:T(8,128)(2,1)}, u32[]{:S(2)}, u32[]{:S(2)}) collective-permute-start(bf16[400,3200]{1,0:T(8,128)(2,1)} %collective-permute-done.7), channel_id=1, source_target_pairs={{0,2},{2,0},{4,6},{6,4},{8,10},{10,8},{12,14},{14,12},{16,18},{18,... | collective-permute-start | bytes 7680008 | tf_op jit(solution)/shard_map/ppermute | solution.py:279
  274.4 37.2 %collective-permute-start.6 = (bf16[512,1600]{0,1:T(8,128)(2,1)}, bf16[512,1600]{0,1:T(8,128)(2,1)}, u32[]{:S(2)}, u32[]{:S(2)}) collective-permute-start(bf16[512,1600]{0,1:T(8,128)(2,1)} %add_convert_fusion.3), channel_id=1, source_target_pairs={{0,1},{1,0},{2,3},{3,2},{4,5},{5,4},{6,7},{7,6},{8,9},{9,8},{10,11... | collective-permute-start | bytes 4915208 | tf_op jit(solution)/shard_map/ppermute | solution.py:276
  377.4 85.4 %collective-permute-start.11 = (bf16[512,1600]{0,1:T(8,128)(2,1)}, bf16[512,1600]{0,1:T(8,128)(2,1)}, u32[]{:S(2)}, u32[]{:S(2)}) collective-permute-start(bf16[512,1600]{0,1:T(8,128)(2,1)} %fusion.46), channel_id=1, source_target_pairs={{0,1},{1,0},{2,3},{3,2},{4,5},{5,4},{6,7},{7,6},{8,9},{9,8},{10,11... | collective-permute-start | bytes 4915208 | tf_op jit(solution)/shard_map/ppermute | solution.py:276
  387.5 89.9 %collective-permute-start.9 = (bf16[512,1600]{0,1:T(8,128)(2,1)}, bf16[512,1600]{0,1:T(8,128)(2,1)}, u32[]{:S(2)}, u32[]{:S(2)}) collective-permute-start(bf16[512,1600]{0,1:T(8,128)(2,1)} %fusion.43), channel_id=1, source_target_pairs={{0,1},{1,0},{2,3},{3,2},{4,5},{5,4},{6,7},{7,6},{8,9},{9,8},{10,11... | collective-permute-start | bytes 4915208 | tf_op jit(solution)/shard_map/ppermute | solution.py:276
  425.4 317.2 %collective-permute-start.25 = (bf16[4,400,1600]{2,1,0:T(8,128)(2,1)}, bf16[4,400,1600]{2,1,0:T(8,128)(2,1)}, u32[]{:S(2)}, u32[]{:S(2)}) collective-permute-start(bf16[4,400,1600]{2,1,0:T(8,128)(2,1)} %dynamic-slice_bitcast_fusion), channel_id=1, source_target_pairs={{0,2},{2,0},{4,6},{6,4},{8,10},{10,8},{12,14},{14,12},{16,18},{18,... | collective-permute-start | bytes 15360008 | tf_op jit(solution)/shard_map/ppermute | solution.py:279
  497.1 23.1 %collective-permute-start.12 = (bf16[512,896]{1,0:T(8,128)(2,1)}, bf16[512,896]{1,0:T(8,128)(2,1)}, u32[]{:S(2)}, u32[]{:S(2)}) collective-permute-start(bf16[512,896]{1,0:T(8,128)(2,1)} %get-tuple-element.100), channel_id=1, source_target_pairs={{0,1},{1,0},{2,3},{3,2},{4,5},{5,4},{6,7},{7,6},{8,9},{9,8},{10,11... | collective-permute-start | bytes 2752520 | tf_op jit(solution)/shard_map/ppermute | solution.py:276
  503.6 254.9 %collective-permute-start.30 = (bf16[8,100,3200]{2,0,1:T(8,128)(2,1)}, bf16[8,100,3200]{2,0,1:T(8,128)(2,1)}, u32[]{:S(2)}, u32[]{:S(2)}) collective-permute-start(bf16[8,100,3200]{2,0,1:T(8,128)(2,1)} %bitcast.215), channel_id=1, source_target_pairs={{0,2},{2,0},{4,6},{6,4},{8,10},{10,8},{12,14},{14,12},{16,18},{18,... | collective-permute-start | bytes 15360008 | tf_op jit(solution)/shard_map/ppermute | solution.py:279
  571.3 37.9 %collective-permute-start.13 = (bf16[512,1600]{0,1:T(8,128)(2,1)}, bf16[512,1600]{0,1:T(8,128)(2,1)}, u32[]{:S(2)}, u32[]{:S(2)}) collective-permute-start(bf16[512,1600]{0,1:T(8,128)(2,1)} %convolution_convert_fusion.6), channel_id=1, source_target_pairs={{0,1},{1,0},{2,3},{3,2},{4,5},{5,4},{6,7},{7,6},{8,9},{9,8},{10,11... | collective-permute-start | bytes 4915208 | tf_op jit(solution)/shard_map/ppermute | solution.py:276
  573.4 45.3 %collective-permute-start.20 = (bf16[8,100,1600]{2,0,1:T(8,128)(2,1)}, bf16[8,100,1600]{2,0,1:T(8,128)(2,1)}, u32[]{:S(2)}, u32[]{:S(2)}) collective-permute-start(bf16[8,100,1600]{2,0,1:T(8,128)(2,1)} %bitcast.216), channel_id=1, source_target_pairs={{0,2},{2,0},{4,6},{6,4},{8,10},{10,8},{12,14},{14,12},{16,18},{18,... | collective-permute-start | bytes 7680008 | tf_op jit(solution)/shard_map/ppermute | solution.py:279
  584.4 187.9 %collective-permute-start.14 = (bf16[800,2688]{1,0:T(8,128)(2,1)}, bf16[800,2688]{1,0:T(8,128)(2,1)}, u32[]{:S(2)}, u32[]{:S(2)}) collective-permute-start(bf16[800,2688]{1,0:T(8,128)(2,1)} %convolution_convert_fusion.4), channel_id=1, source_target_pairs={{0,2},{2,0},{4,6},{6,4},{8,10},{10,8},{12,14},{14,12},{16,18},{18,... | collective-permute-start | bytes 12902408 | tf_op jit(solution)/shard_map/ppermute | solution.py:279
  625.2 126.1 %collective-permute-start.21 = (bf16[4,100,1600]{2,0,1:T(4,128)(2,1)}, bf16[4,100,1600]{2,0,1:T(4,128)(2,1)}, u32[]{:S(2)}, u32[]{:S(2)}) collective-permute-start(bf16[4,100,1600]{2,0,1:T(4,128)(2,1)} %bitcast.218), channel_id=1, source_target_pairs={{0,4},{2,6},{4,0},{6,2},{8,12},{10,14},{12,8},{14,10},{16,20},{18,... | collective-permute-start | bytes 3840008 | tf_op jit(solution)/shard_map/ppermute | solution.py:279
  749.8 60.7 %collective-permute-start.26 = (bf16[2,400,1600]{2,1,0:T(8,128)(2,1)}, bf16[2,400,1600]{2,1,0:T(8,128)(2,1)}, u32[]{:S(2)}, u32[]{:S(2)}) collective-permute-start(bf16[2,400,1600]{2,1,0:T(8,128)(2,1)} %dynamic-slice_bitcast_fusion.2), channel_id=1, source_target_pairs={{0,4},{2,6},{4,0},{6,2},{8,12},{10,14},{12,8},{14,10},{16,20},{18,... | collective-permute-start | bytes 7680008 | tf_op jit(solution)/shard_map/ppermute | solution.py:279
  780.1 48.7 %collective-permute-start.15 = (bf16[400,2688]{1,0:T(8,128)(2,1)S(1)}, bf16[400,2688]{1,0:T(8,128)(2,1)S(1)}, u32[]{:S(2)}, u32[]{:S(2)}) collective-permute-start(bf16[400,2688]{1,0:T(8,128)(2,1)S(1)} %dynamic-slice_bitcast_fusion.4), channel_id=1, source_target_pairs={{0,1},{1,0},{2,3},{3,2},{4,5},{5,4},{6,7},{7,6},{8,9},{9,8},{10,11... | collective-permute-start | bytes 6451208 | tf_op jit(solution)/shard_map/ppermute | solution.py:276
  785.9 93.9 %collective-permute-start.31 = (bf16[4,100,3200]{2,0,1:T(4,128)(2,1)}, bf16[4,100,3200]{2,0,1:T(4,128)(2,1)}, u32[]{:S(2)}, u32[]{:S(2)}) collective-permute-start(bf16[4,100,3200]{2,0,1:T(4,128)(2,1)} %bitcast.217), channel_id=1, source_target_pairs={{0,4},{2,6},{4,0},{6,2},{8,12},{10,14},{12,8},{14,10},{16,20},{18,... | collective-permute-start | bytes 7680008 | tf_op jit(solution)/shard_map/ppermute | solution.py:279
  797.6 87.3 %collective-permute-start.24 = (bf16[100,800]{1,0:T(8,128)(2,1)}, bf16[100,800]{1,0:T(8,128)(2,1)S(1)}, u32[]{:S(2)}, u32[]{:S(2)}) collective-permute-start(bf16[100,800]{1,0:T(8,128)(2,1)} %dynamic-slice_bitcast_fusion.9), channel_id=1, source_target_pairs={{0,1},{1,0},{2,3},{3,2},{4,5},{5,4},{6,7},{7,6},{8,9},{9,8},{10,11... | collective-permute-start | bytes 480008 | tf_op jit(solution)/shard_map/ppermute | solution.py:276
  814.2 71.7 %collective-permute-start.27 = (bf16[1,400,1600]{2,1,0:T(8,128)(2,1)}, bf16[1,400,1600]{2,1,0:T(8,128)(2,1)}, u32[]{:S(2)}, u32[]{:S(2)}) collective-permute-start(bf16[1,400,1600]{2,1,0:T(8,128)(2,1)} %constant_dynamic-slice_fusion.3), channel_id=1, source_target_pairs={{0,8},{2,10},{4,12},{6,14},{8,0},{10,2},{12,4},{14,6},{16,24},{18,... | collective-permute-start | bytes 3840008 | tf_op jit(solution)/shard_map/ppermute | solution.py:279
  878.3 41.9 %collective-permute-start.16 = (bf16[4,400,600]{2,1,0:T(8,128)(2,1)}, bf16[4,400,600]{2,1,0:T(8,128)(2,1)}, u32[]{:S(2)}, u32[]{:S(2)}) collective-permute-start(bf16[4,400,600]{2,1,0:T(8,128)(2,1)} %bitcast.260), channel_id=1, source_target_pairs={{0,4},{2,6},{4,0},{6,2},{8,12},{10,14},{12,8},{14,10},{16,20},{18,... | collective-permute-start | bytes 5760008 | tf_op jit(solution)/shard_map/ppermute | solution.py:279
  884.9 38.1 %collective-permute-start.32 = (bf16[2,100,3200]{2,0,1:T(2,128)(2,1)}, bf16[2,100,3200]{2,0,1:T(2,128)(2,1)}, u32[]{:S(2)}, u32[]{:S(2)}) collective-permute-start(bf16[2,100,3200]{2,0,1:T(2,128)(2,1)} %copy.133), channel_id=1, source_target_pairs={{0,8},{2,10},{4,12},{6,14},{8,0},{10,2},{12,4},{14,6},{16,24},{18,... | collective-permute-start | bytes 3840008 | tf_op jit(solution)/shard_map/ppermute | solution.py:279
  888.5 37.9 %collective-permute-start.28 = (bf16[400,800]{1,0:T(8,128)(2,1)S(1)}, bf16[400,800]{1,0:T(8,128)(2,1)}, u32[]{:S(2)}, u32[]{:S(2)}) collective-permute-start(bf16[400,800]{1,0:T(8,128)(2,1)S(1)} %dynamic-slice_bitcast_fusion.7), channel_id=1, source_target_pairs={{0,1},{1,0},{2,3},{3,2},{4,5},{5,4},{6,7},{7,6},{8,9},{9,8},{10,11... | collective-permute-start | bytes 1920008 | tf_op jit(solution)/shard_map/ppermute | solution.py:276
  923.0 39.2 %collective-permute-start.17 = (bf16[2,400,600]{2,1,0:T(8,128)(2,1)S(1)}, bf16[2,400,600]{2,1,0:T(8,128)(2,1)S(1)}, u32[]{:S(2)}, u32[]{:S(2)}) collective-permute-start(bf16[2,400,600]{2,1,0:T(8,128)(2,1)S(1)} %dynamic-slice_bitcast_fusion.6), channel_id=1, source_target_pairs={{0,8},{2,10},{4,12},{6,14},{8,0},{10,2},{12,4},{14,6},{16,24},{18,... | collective-permute-start | bytes 2880008 | tf_op jit(solution)/shard_map/ppermute | solution.py:279
  924.8 59.5 %collective-permute-start.33 = (bf16[1,100,3200]{2,1,0:T(8,128)(2,1)S(1)}, bf16[1,100,3200]{2,1,0:T(8,128)(2,1)S(1)}, u32[]{:S(2)}, u32[]{:S(2)}) collective-permute-start(bf16[1,100,3200]{2,1,0:T(8,128)(2,1)S(1)} %constant_dynamic-slice_fusion), channel_id=1, source_target_pairs={{0,16},{2,18},{4,20},{6,22},{8,24},{10,26},{12,28},{14,30},{16,0},... | collective-permute-start | bytes 1920008 | tf_op jit(solution)/shard_map/ppermute | solution.py:279
  929.3 76.7 %collective-permute-start.29 = (bf16[1,400,800]{2,1,0:T(8,128)(2,1)}, bf16[1,400,800]{2,1,0:T(8,128)(2,1)}, u32[]{:S(2)}, u32[]{:S(2)}) collective-permute-start(bf16[1,400,800]{2,1,0:T(8,128)(2,1)} %fusion.59), channel_id=1, source_target_pairs={{0,16},{2,18},{4,20},{6,22},{8,24},{10,26},{12,28},{14,30},{16,0},... | collective-permute-start | bytes 1920008 | tf_op jit(solution)/shard_map/ppermute | solution.py:279
  962.5 41.3 %collective-permute-start.18 = (bf16[1,400,600]{2,1,0:T(8,128)(2,1)S(1)}, bf16[1,400,600]{2,1,0:T(8,128)(2,1)S(1)}, u32[]{:S(2)}, u32[]{:S(2)}) collective-permute-start(bf16[1,400,600]{2,1,0:T(8,128)(2,1)S(1)} %constant_dynamic-slice_fusion.9), channel_id=1, source_target_pairs={{0,16},{2,18},{4,20},{6,22},{8,24},{10,26},{12,28},{14,30},{16,0},... | collective-permute-start | bytes 1440008 | tf_op jit(solution)/shard_map/ppermute | solution.py:279
  (66 other events, 1045.2 us)
Sparse Core Ops, SparseCore 0:
  618.8 119.5 all-reduce.9
